TPU v7x, 32 devices: a whole 2x2x4 slice. The times are simulated.
32 devices in a mesh: fsdp: 8 (over z, y), ctx: 4 (over x, core).
Axes of the slice: x: 2, y: 2, z: 4, core: 2. Of those that a mesh axis runs over, the one named last changes fastest.
Arguments:
- hidden: bfloat16 [8, 1024, 8192], P('fsdp', 'ctx'), may hold values from -400 to 400
- norm_gain: bfloat16 [8192], replicated, may hold values from 0.099609375 to 1.8984375
- w_query: bfloat16 [8192, 1024], P('fsdp'), may hold values from -0.109375 to 0.109375
- w_key: bfloat16 [8192, 128], P('fsdp'), may hold values from -0.109375 to 0.109375
- w_value: bfloat16 [8192, 128], P('fsdp'), may hold values from -0.0625 to 0.0625
- bias_query: bfloat16 [1024], replicated, may hold values from -24 to 24
- bias_key: bfloat16 [128], replicated, may hold values from -9 to 9
- bias_value: bfloat16 [128], replicated, may hold values from -3 to 3
Outputs:
- attended: bfloat16 [8, 1024, 1024], P('fsdp', 'ctx')
All inputs are finite; a program needn't handle non-finite values.
Results may differ from a plain program's by a relative error of at most 0.012.
Values may be sent and summed in bfloat16 or wider, within the bound.
No kernel may reach another device: no remote copies, remote signals or barrier semaphores. Data moves between devices by JAX's collectives and lax.ppermute only.
A program may use at most 128 MiB of HBM per device.

v0:
```python
import math
import jax
import jax.numpy as jnp
from jax import lax
from jax.sharding import PartitionSpec as P

epsilon = 1e-06
rotary_base = 1000000.0
masked_score = -1e30


def shifted(value, axis, steps):
    count = lax.axis_size(axis)
    first, last = (max(0, -steps), min(count, count - steps))
    return lax.ppermute(value, axis, [(source, source + steps) for source in range(first, last)])


def rotary_tables(positions, head_width):
    half_width = head_width // 2
    frequency = jnp.exp(
        -(jnp.arange(half_width, dtype=jnp.float32) * (2.0 / head_width)) * math.log(rotary_base)
    )
    angles = positions.astype(jnp.float32)[:, None] * frequency[None, :]
    return (jnp.cos(angles)[:, None, :], jnp.sin(angles)[:, None, :])


def rotate(tensor, cosine, sine_table):
    half_width = tensor.shape[-1] // 2
    lower_half = tensor[..., :half_width]
    upper_half = tensor[..., half_width:]
    return jnp.concatenate(
        [
            lower_half * cosine - upper_half * sine_table,
            upper_half * cosine + lower_half * sine_table,
        ],
        axis=-1,
    )


def normalize(inputs, norm_gain):
    floats = inputs.astype(jnp.float32)
    scaled = floats * lax.rsqrt(jnp.mean(floats * floats, axis=-1, keepdims=True) + epsilon)
    return (scaled * norm_gain.astype(jnp.float32)).astype(jnp.bfloat16)


def contract_rows(operand, pieces):
    return tuple((jnp.dot(operand, piece, preferred_element_type=jnp.float32) for piece in pieces))


def attend(work_queries, score_scale, running, key_value, visible):
    row_peak, row_total, weighted = running
    scores = (
        jnp.einsum("qhd,kd->hqk", work_queries, key_value[0], preferred_element_type=jnp.float32)
        * score_scale
    )
    scores = jnp.where(visible, scores, masked_score)
    new_peak = jnp.maximum(row_peak, jnp.max(scores, axis=-1))
    factor = jnp.exp(row_peak - new_peak)
    expsum = jnp.exp(scores - new_peak[..., None])
    row_total = row_total * factor + jnp.sum(expsum, axis=-1)
    weights = expsum.astype(jnp.bfloat16)
    weighted = weighted * factor[..., None] + jnp.einsum(
        "hqk,kd->hqd", weights, key_value[1], preferred_element_type=jnp.float32
    )
    return (new_peak, row_total, weighted)


def shards(hidden, norm_gain, w_query, w_key, w_value, bias_query, bias_key, bias_value):
    local_rows = hidden.shape[1]
    head_width = w_key.shape[1]
    query_width = w_query.shape[1]
    query_heads = query_width // head_width
    normed = normalize(hidden[0], norm_gain)
    sums = contract_rows(
        normed,
        (
            lax.all_gather(w_query, "fsdp", axis=0, tiled=True),
            lax.all_gather(w_key, "fsdp", axis=0, tiled=True),
            lax.all_gather(w_value, "fsdp", axis=0, tiled=True),
        ),
    )
    query_sums, key_sums, value_sums = sums
    slab_index = lax.axis_index("ctx")
    slab_count = lax.axis_size("ctx")
    positions = slab_index * local_rows + jnp.arange(local_rows, dtype=jnp.int32)
    cosine, sine_table = rotary_tables(positions, head_width)
    queries = rotate(
        (query_sums + bias_query.astype(jnp.float32)).reshape(local_rows, query_heads, head_width),
        cosine,
        sine_table,
    ).astype(jnp.bfloat16)
    keys = rotate((key_sums + bias_key.astype(jnp.float32))[:, None, :], cosine, sine_table)[
        :, 0, :
    ].astype(jnp.bfloat16)
    values = (value_sums + bias_value.astype(jnp.float32)).astype(jnp.bfloat16)
    score_scale = head_width ** (-0.5)
    start_state = (
        jnp.full((query_heads, local_rows), masked_score, jnp.float32),
        jnp.zeros((query_heads, local_rows), jnp.float32),
        jnp.zeros((query_heads, local_rows, head_width), jnp.float32),
    )
    key_value = jnp.stack([keys, values])
    column_ids = jnp.arange(local_rows, dtype=jnp.int32)
    causal = column_ids[None, :] <= column_ids[:, None]
    running = attend(queries, score_scale, start_state, key_value, causal[None])

    def forward_step(step_number, state):
        held_running, blocks = state
        blocks = shifted(blocks, "ctx", 1)
        visible = step_number <= slab_index
        held_running = attend(queries, score_scale, held_running, blocks, visible)
        return (held_running, blocks)

    running, key_value = lax.fori_loop(1, slab_count, forward_step, (running, key_value))
    row_peak, row_total, weighted = running
    attended = (
        (weighted / row_total[..., None])
        .transpose(1, 0, 2)
        .reshape(local_rows, query_width)
        .astype(jnp.bfloat16)
    )
    return attended[None]


def solution(mesh):
    in_specs = (
        P("fsdp", "ctx", None),
        P(),
        P("fsdp", None),
        P("fsdp", None),
        P("fsdp", None),
        P(),
        P(),
        P(),
    )
    out_specs = P("fsdp", "ctx", None)
    return jax.shard_map(shards, mesh=mesh, in_specs=in_specs, out_specs=out_specs, check_vma=False)
```

profile of v0, /device:TPU:1, one launch (start us, length us, event | category | flops | bytes accessed | tf_op | source)
XLA Modules:
  0.0 384.0 jit_solution(6353027936937991859)
XLA Ops:
  6.6 0.7 all-gather.4.cloned.1.call-update
  7.3 0.7 all-gather.8.cloned.1.call-update
  8.1 0.7 all-gather.6.cloned.1.call-update
  8.9 3.1 fusion.11
  12.0 0.5 multiply_cosine_fusion
  12.6 47.2 %all-gather.4.cloned.1.call-done = bf16[8192,128]{1,0:T(8,128)(2,1)} async-done(((bf16[1024,128]{1,0:T(8,128)(2,1)}), bf16[8192,128]{1,0:T(8,128)(2,1)}) %all-gather.4.cloned.1.call-update) | async-done | bytes 2097168 | tf_op jit(solution)/shard_map/all_gather | solution.py:78
  59.8 4.6 %fusion.17 = f32[256,1,128]{0,2,1:T(8,128)S(1)} fusion(bf16[8192,128]{1,0:T(8,128)(2,1)} %all-gather.4.cloned.1.call-done, f32[128]{0:T(128)S(1)} %convert_element_type.78, bf16[1,256,8192]{2,1,0:T(8,128)(2,1)} %param.10, f32[8192]{0:T(1024)S(1)} %convert_element_type.76, f32[256]{0:T(256)S(1)} %add_rsqrt_fusion), kind=kOutput, calls=%fused_computation.32 | convolution fusion | flops 545292288 | bytes 6456832 | tf_op jit(solution)/shard_map/dot_general | solution.py:47
  64.8 45.0 %all-gather.8.cloned.1.call-done = bf16[8192,128]{1,0:T(8,128)(2,1)} async-done(((bf16[1024,128]{1,0:T(8,128)(2,1)}), bf16[8192,128]{1,0:T(8,128)(2,1)}) %all-gather.8.cloned.1.call-update) | async-done | bytes 2097168 | tf_op jit(solution)/shard_map/all_gather | solution.py:79
  109.7 4.6 %fusion.18 = bf16[256,128]{0,1:T(8,128)(2,1)S(1)} fusion(bf16[8192,128]{1,0:T(8,128)(2,1)} %all-gather.8.cloned.1.call-done, f32[128]{0:T(128)S(1)} %convert_element_type.84, bf16[1,256,8192]{2,1,0:T(8,128)(2,1)} %param.10, f32[8192]{0:T(1024)S(1)} %convert_element_type.76, f32[256]{0:T(256)S(1)} %add_rsqrt_fusion), kind=kOutput, calls=%fused_computation.33 | convolution fusion | flops 545325056 | bytes 6391296 | tf_op jit(solution)/shard_map/dot_general | solution.py:47
  114.5 224.2 %all-gather.6.cloned.1.call-done = bf16[8192,1024]{1,0:T(8,128)(2,1)} async-done(((bf16[1024,1024]{1,0:T(8,128)(2,1)}), bf16[8192,1024]{1,0:T(8,128)(2,1)}) %all-gather.6.cloned.1.call-update) | async-done | bytes 16777232 | tf_op jit(solution)/shard_map/all_gather | solution.py:77
  338.7 9.6 %fusion.16 = f32[32,8,8,128]{3,1,2,0:T(8,128)S(1)} fusion(bf16[8192,1024]{1,0:T(8,128)(2,1)} %all-gather.6.cloned.1.call-done, f32[1024]{0:T(1024)S(1)} %convert_element_type.82, bf16[1,256,8192]{2,1,0:T(8,128)(2,1)} %param.10, f32[8192]{0:T(1024)S(1)} %convert_element_type.76, f32[256]{0:T(256)S(1)} %add_rsqrt_fusion), kind=kOutput, calls=%fused_computation.28 | convolution fusion | flops 4303618048 | bytes 22057984 | tf_op jit(solution)/shard_map/dot_general | solution.py:47
  349.5 0.5 fusion.37
  350.4 0.8 convolution_add_fusion.2
  351.2 24.6 %while.19 = (s32[]{:T(128)}, f32[8,256]{1,0:T(8,128)S(1)}, f32[8,256]{1,0:T(8,128)S(1)}, f32[8,256,128]{2,1,0:T(8,128)S(1)}, bf16[2,256,128]{2,1,0:T(8,128)(2,1)...) while((s32[]{:T(128)}, f32[8,256]{1,0:T(8,128)S(1)}, f32[8,256]{1,0:T(8,128)S(1)}, ...), condition=%wide.region_6.7_spmd, body=%wide.region_3.6_spmd.sunk | while | flops 274731008 | bytes 9961609 | solution.py:114
  351.2 4.0 %collective-permute-start = (bf16[2,256,128]{2,1,0:T(8,128)(2,1)S(1)}, bf16[2,256,128]{2,1,0:T(8,128)(2,1)S(1)}, u32[]{:S(2)}, u32[]{:S(2)}) collective-permute-start(bf16[2,256,128]{2,1,0:T(8,128)(2,1)S(1)} %get-tuple-element.232), channel_id=1, source_target_pairs={{0,1},{1,2},{2,3},{4,5},{5,6},{6,7},{8,9},{9,10},{10,11},{12,13},{... | collective-permute-start | bytes 393224 | tf_op jit(solution)/shard_map/while/body/eval_jaxpr/ppermute | solution.py:15
  355.2 1.9 collective-permute-done
  358.1 1.0 convolution_add_fusion.6
  359.1 4.4 %collective-permute-start = (bf16[2,256,128]{2,1,0:T(8,128)(2,1)S(1)}, bf16[2,256,128]{2,1,0:T(8,128)(2,1)S(1)}, u32[]{:S(2)}, u32[]{:S(2)}) collective-permute-start(bf16[2,256,128]{2,1,0:T(8,128)(2,1)S(1)} %get-tuple-element.232), channel_id=1, source_target_pairs={{0,1},{1,2},{2,3},{4,5},{5,6},{6,7},{8,9},{9,10},{10,11},{12,13},{... | collective-permute-start | bytes 393224 | tf_op jit(solution)/shard_map/while/body/eval_jaxpr/ppermute | solution.py:15
  363.5 1.9 collective-permute-done
  366.4 1.0 convolution_add_fusion.6
  367.5 4.4 %collective-permute-start = (bf16[2,256,128]{2,1,0:T(8,128)(2,1)S(1)}, bf16[2,256,128]{2,1,0:T(8,128)(2,1)S(1)}, u32[]{:S(2)}, u32[]{:S(2)}) collective-permute-start(bf16[2,256,128]{2,1,0:T(8,128)(2,1)S(1)} %get-tuple-element.232), channel_id=1, source_target_pairs={{0,1},{1,2},{2,3},{4,5},{5,6},{6,7},{8,9},{9,10},{10,11},{12,13},{... | collective-permute-start | bytes 393224 | tf_op jit(solution)/shard_map/while/body/eval_jaxpr/ppermute | solution.py:15
  371.8 1.9 collective-permute-done
  374.7 1.0 convolution_add_fusion.6
  376.5 1.0 convert_element_type.89
  (50 shorter events, 5.6 us)
Async XLA Ops:
  6.5 2.2 copy-start
  6.5 2.2 copy-start.1
  6.5 2.3 copy-start.2
  6.5 2.3 copy-start.3
  6.5 53.3 %all-gather.4.cloned.1.call-start = ((), (), s32[]{:S(2)}) async-start(), calls=%async_computation | async-start | bytes 2359296 | tf_op jit(solution)/shard_map/all_gather | solution.py:78
  7.3 102.5 %all-gather.8.cloned.1.call-start = ((), (), s32[]{:S(2)}) async-start(), calls=%async_computation.2 | async-start | bytes 2359296 | tf_op jit(solution)/shard_map/all_gather | solution.py:79
  8.0 330.7 %all-gather.6.cloned.1.call-start = ((), (), s32[]{:S(2)}) async-start(), calls=%async_computation.1 | async-start | bytes 18874368 | tf_op jit(solution)/shard_map/all_gather | solution.py:77
  351.2 6.0 %collective-permute-start = (bf16[2,256,128]{2,1,0:T(8,128)(2,1)S(1)}, bf16[2,256,128]{2,1,0:T(8,128)(2,1)S(1)}, u32[]{:S(2)}, u32[]{:S(2)}) collective-permute-start(bf16[2,256,128]{2,1,0:T(8,128)(2,1)S(1)} %get-tuple-element.232), channel_id=1, source_target_pairs={{0,1},{1,2},{2,3},{4,5},{5,6},{6,7},{8,9},{9,10},{10,11},{12,13},{... | collective-permute-start | bytes 393224 | tf_op jit(solution)/shard_map/while/body/eval_jaxpr/ppermute | solution.py:15
  359.1 6.3 %collective-permute-start = (bf16[2,256,128]{2,1,0:T(8,128)(2,1)S(1)}, bf16[2,256,128]{2,1,0:T(8,128)(2,1)S(1)}, u32[]{:S(2)}, u32[]{:S(2)}) collective-permute-start(bf16[2,256,128]{2,1,0:T(8,128)(2,1)S(1)} %get-tuple-element.232), channel_id=1, source_target_pairs={{0,1},{1,2},{2,3},{4,5},{5,6},{6,7},{8,9},{9,10},{10,11},{12,13},{... | collective-permute-start | bytes 393224 | tf_op jit(solution)/shard_map/while/body/eval_jaxpr/ppermute | solution.py:15
  367.5 6.3 %collective-permute-start = (bf16[2,256,128]{2,1,0:T(8,128)(2,1)S(1)}, bf16[2,256,128]{2,1,0:T(8,128)(2,1)S(1)}, u32[]{:S(2)}, u32[]{:S(2)}) collective-permute-start(bf16[2,256,128]{2,1,0:T(8,128)(2,1)S(1)} %get-tuple-element.232), channel_id=1, source_target_pairs={{0,1},{1,2},{2,3},{4,5},{5,6},{6,7},{8,9},{9,10},{10,11},{12,13},{... | collective-permute-start | bytes 393224 | tf_op jit(solution)/shard_map/while/body/eval_jaxpr/ppermute | solution.py:15
Sparse Core Ops, SparseCore 0:
  9.5 50.2 all-gather.3
  61.9 47.7 all-gather.7
  111.9 226.7 all-gather.5
where the time goes:
time: 384 us
  waiting for transfers between devices  324 us (84%)
  matrix products  24.5 us (6%)
  between operations  13.3 us (3%)
  starting transfers between devices  12.9 us (3%)
  other arithmetic  6.76 us (2%)
    all_gather x1, waiting for transfers between devices, shards(): lax.all_gather(w_query, 'fsdp', axis=0, tiled=True)  224 us
    all_gather x1, waiting for transfers between devices, shards(): lax.all_gather(w_key, 'fsdp', axis=0, tiled=True)  47.2 us
    all_gather x1, waiting for transfers between devices, shards(): lax.all_gather(w_value, 'fsdp', axis=0, tiled=True)  45 us
    dot_general x3, matrix products, contract_rows(): jnp.dot(operand, piece, preferred_element_type=jnp.float32)  18.8 us
    ppermute x3, starting transfers between devices, shifted(): lax.ppermute(value, axis, [(source, source + steps) for source in range(f...  12.8 us
  transfers between devices with their start and end apart: 6, of which 6 were waited for; matrix products, arithmetic and copies ran while one was open for 3% of the time, Pallas kernels for 0%

commit v1 on v0

--- a/solution.py
+++ b/solution.py
@@ -7,6 +7,28 @@
 epsilon = 1e-06
 rotary_base = 1000000.0
 masked_score = -1e30
+
+
+def joined_along(blocks, dim):
+    shape = list(blocks.shape[1:])
+    shape[dim] *= blocks.shape[0]
+    return jnp.moveaxis(blocks, 0, dim).reshape(shape)
+
+
+def collect(x, axis, dim):
+    peers = lax.axis_size(axis)
+    pairs = [(i, (i + 1) % peers) for i in range(peers)]
+    back = [(b, a) for a, b in pairs]
+    lower, upper = ([], [])
+    for step in range(peers - 1):
+        if step % 2 == 0:
+            lower.append(lax.ppermute(lower[-1] if lower else x, axis, pairs))
+        else:
+            upper.append(lax.ppermute(upper[-1] if upper else x, axis, back))
+    parts = jnp.stack([*lower[::-1], x, *upper])
+    shift = lax.axis_index(axis) - len(lower)
+    parts = parts[(jnp.arange(peers) - shift) % peers]
+    return joined_along(parts, dim)
 
 
 def shifted(value, axis, steps):
@@ -76,7 +98,7 @@
         (
             lax.all_gather(w_query, "fsdp", axis=0, tiled=True),
             lax.all_gather(w_key, "fsdp", axis=0, tiled=True),
-            lax.all_gather(w_value, "fsdp", axis=0, tiled=True),
+            collect(w_value, "fsdp", 0),
         ),
     )
     query_sums, key_sums, value_sums = sums

time: 384 us -> 355 us (0.924)
  waiting for transfers between devices: 324 us -> 266 us
  starting transfers between devices: 12.9 us -> 36.6 us
  local copies, waits for them, and re-layouts: 2.07 us -> 7.34 us
    all_gather x1, waiting for transfers between devices: 47.2 us -> 0.32 us  [shards(): lax.all_gather(w_key, 'fsdp', axis=0, tiled=True)]
    all_gather x1 -> x0, waiting for transfers between devices: 45 us -> none  [shards(): lax.all_gather(w_value, 'fsdp', axis=0, tiled=True)]
    ppermute x0 -> x7, waiting for transfers between devices: none -> 34.1 us  [the longest x4 33.8 us: collect(): lower.append(lax.ppermute(lower[-1] if lower else x, axis, pairs))]
    ppermute x0 -> x7, starting transfers between devices: none -> 23.8 us  [the longest x3 16.5 us: collect(): upper.append(lax.ppermute(upper[-1] if upper else x, axis, back))]
  transfers between devices with their start and end apart: 6 -> 12, of which waited for: 6 -> 10; matrix products, arithmetic and copies ran while one was open for 3% -> 5% of each run, Pallas kernels for 0% -> 0%
where the time goes in v1:
time: 355 us
  waiting for transfers between devices  266 us (75%)
  starting transfers between devices  36.6 us (10%)
  matrix products  24.5 us (7%)
  between operations  13.7 us (4%)
  local copies, waits for them, and re-layouts  7.34 us (2%)
  other arithmetic  6.78 us (2%)
    all_gather x1, waiting for transfers between devices, shards(): lax.all_gather(w_query, 'fsdp', axis=0, tiled=True)  224 us
    ppermute x4, waiting for transfers between devices, collect(): lower.append(lax.ppermute(lower[-1] if lower else x, axis, pairs))  33.8 us
    dot_general x3, matrix products, contract_rows(): jnp.dot(operand, piece, preferred_element_type=jnp.float32)  18.8 us
    ppermute x3, starting transfers between devices, collect(): upper.append(lax.ppermute(upper[-1] if upper else x, axis, back))  16.5 us
    ppermute x3, starting transfers between devices, shifted(): lax.ppermute(value, axis, [(source, source + steps) for source in range(f...  12.8 us
    ppermute x4, starting transfers between devices, collect(): lower.append(lax.ppermute(lower[-1] if lower else x, axis, pairs))  7.33 us
  transfers between devices with their start and end apart: 12, of which 10 were waited for; matrix products, arithmetic and copies ran while one was open for 5% of the time, Pallas kernels for 0%

profile of v1, /device:TPU:1, one launch (start us, length us, event | category | flops | bytes accessed | tf_op | source)
XLA Modules:
  0.0 354.9 jit_solution(656343743816649998)
XLA Ops:
  8.0 2.1 collective-permute-start.1
  10.1 3.1 collective-permute-start.5
  13.4 7.6 %collective-permute-done.1 = bf16[1024,128]{1,0:T(8,128)(2,1)S(1)} collective-permute-done((bf16[1024,128]{1,0:T(8,128)(2,1)S(1)}, bf16[1024,128]{1,0:T(8,128)(2,1)S(1)}, u32[]{:S(2)}, u32[]{:S(2)}) %collective-permute-start.1) | collective-permute-done | bytes 262176 | tf_op jit(solution)/shard_map/ppermute | solution.py:25
  21.0 2.3 collective-permute-start.2
  23.3 3.1 fusion.13
  26.4 10.7 %collective-permute-done.2 = bf16[1024,128]{1,0:T(8,128)(2,1)S(1)} collective-permute-done((bf16[1024,128]{1,0:T(8,128)(2,1)S(1)}, bf16[1024,128]{1,0:T(8,128)(2,1)S(1)}, u32[]{:S(2)}, u32[]{:S(2)}) %collective-permute-start.2) | collective-permute-done | bytes 262176 | tf_op jit(solution)/shard_map/ppermute | solution.py:25
  37.1 4.2 %collective-permute-start.6 = (bf16[1024,128]{1,0:T(8,128)(2,1)S(1)}, bf16[1024,128]{1,0:T(8,128)(2,1)}, u32[]{:S(2)}, u32[]{:S(2)}) collective-permute-start(bf16[1024,128]{1,0:T(8,128)(2,1)S(1)} %collective-permute-done.5), channel_id=1, source_target_pairs={{4,0},{8,4},{12,8},{16,12},{20,16},{24,20},{28,24},{0,28},{5,1},{9... | collective-permute-start | bytes 786440 | tf_op jit(solution)/shard_map/ppermute | solution.py:27
  41.3 8.7 %collective-permute-done.3 = bf16[1024,128]{1,0:T(8,128)(2,1)S(1)} collective-permute-done((bf16[1024,128]{1,0:T(8,128)(2,1)S(1)}, bf16[1024,128]{1,0:T(8,128)(2,1)S(1)}, u32[]{:S(2)}, u32[]{:S(2)}) %collective-permute-start.3) | collective-permute-done | bytes 262176 | tf_op jit(solution)/shard_map/ppermute | solution.py:25
  50.0 2.9 collective-permute-start.4
  53.6 9.2 %collective-permute-start.7 = (bf16[1024,128]{1,0:T(8,128)(2,1)}, bf16[1024,128]{1,0:T(8,128)(2,1)S(1)}, u32[]{:S(2)}, u32[]{:S(2)}) collective-permute-start(bf16[1024,128]{1,0:T(8,128)(2,1)} %collective-permute-done.6), channel_id=1, source_target_pairs={{4,0},{8,4},{12,8},{16,12},{20,16},{24,20},{28,24},{0,28},{5,1},{9... | collective-permute-start | bytes 786440 | tf_op jit(solution)/shard_map/ppermute | solution.py:27
  62.8 6.8 %collective-permute-done.4 = bf16[1024,128]{1,0:T(8,128)(2,1)} collective-permute-done((bf16[1024,128]{1,0:T(8,128)(2,1)S(1)}, bf16[1024,128]{1,0:T(8,128)(2,1)}, u32[]{:S(2)}, u32[]{:S(2)}) %collective-permute-start.4) | collective-permute-done | bytes 262176 | tf_op jit(solution)/shard_map/ppermute | solution.py:25
  73.1 2.1 gather_fusion
  75.2 4.6 %fusion.38 = bf16[256,128]{0,1:T(8,128)(2,1)S(1)} fusion(bf16[8192,128]{1,0:T(8,128)(2,1)} %bitcast.104, bf16[1,256,8192]{2,1,0:T(8,128)(2,1)} %param.10, f32[8192]{0:T(1024)S(1)} %convert_element_type.84, f32[256]{0:T(256)S(1)} %add_rsqrt_fusion, f32[128]{0:T(128)S(1)} %convert_element_type.95), kind=kOutput, calls=%fused_computation.43 | convolution fusion | flops 545325056 | bytes 6391296 | tf_op jit(solution)/shard_map/dot_general | solution.py:69
  80.1 4.6 %fusion.32 = f32[256,1,128]{0,2,1:T(8,128)S(1)} fusion(bf16[8192,128]{1,0:T(8,128)(2,1)} %all-gather.3.cloned.1.call-done, bf16[1,256,8192]{2,1,0:T(8,128)(2,1)} %param.10, f32[8192]{0:T(1024)S(1)} %convert_element_type.84, f32[256]{0:T(256)S(1)} %add_rsqrt_fusion, f32[128]{0:T(128)S(1)} %convert_element_type.86), kind=kOutput, calls=%fused_computation.41 | convolution fusion | flops 545292288 | bytes 6456832 | tf_op jit(solution)/shard_map/dot_general | solution.py:69
  85.3 224.1 %all-gather.5.cloned.1.call-done = bf16[8192,1024]{1,0:T(8,128)(2,1)} async-done(((bf16[1024,1024]{1,0:T(8,128)(2,1)}), bf16[8192,1024]{1,0:T(8,128)(2,1)}) %all-gather.5.cloned.1.call-update) | async-done | bytes 16777232 | tf_op jit(solution)/shard_map/all_gather | solution.py:99
  309.3 9.6 %fusion.25 = f32[32,8,8,128]{3,1,2,0:T(8,128)S(1)} fusion(bf16[8192,1024]{1,0:T(8,128)(2,1)} %all-gather.5.cloned.1.call-done, bf16[1,256,8192]{2,1,0:T(8,128)(2,1)} %param.10, f32[8192]{0:T(1024)S(1)} %convert_element_type.84, f32[256]{0:T(256)S(1)} %add_rsqrt_fusion, f32[1024]{0:T(1024)S(1)} %convert_element_type.90), kind=kOutput, calls=%fused_computation.37 | convolution fusion | flops 4303618048 | bytes 22057984 | tf_op jit(solution)/shard_map/dot_general | solution.py:69
  321.8 24.6 %while.19 = (s32[]{:T(128)}, f32[8,256]{1,0:T(8,128)S(1)}, f32[8,256]{1,0:T(8,128)S(1)}, f32[8,256,128]{2,1,0:T(8,128)S(1)}, bf16[2,256,128]{2,1,0:T(8,128)(2,1)...) while((s32[]{:T(128)}, f32[8,256]{1,0:T(8,128)S(1)}, f32[8,256]{1,0:T(8,128)S(1)}, ...), condition=%wide.region_6.7_spmd, body=%wide.region_3.6_spmd.sunk | while | flops 274731008 | bytes 9961609 | solution.py:136
  321.8 4.0 %collective-permute-start = (bf16[2,256,128]{2,1,0:T(8,128)(2,1)S(1)}, bf16[2,256,128]{2,1,0:T(8,128)(2,1)S(1)}, u32[]{:S(2)}, u32[]{:S(2)}) collective-permute-start(bf16[2,256,128]{2,1,0:T(8,128)(2,1)S(1)} %get-tuple-element.232), channel_id=1, source_target_pairs={{0,1},{1,2},{2,3},{4,5},{5,6},{6,7},{8,9},{9,10},{10,11},{12,13},{... | collective-permute-start | bytes 393224 | tf_op jit(solution)/shard_map/while/body/eval_jaxpr/ppermute | solution.py:37
  325.8 1.9 collective-permute-done
  329.8 4.4 %collective-permute-start = (bf16[2,256,128]{2,1,0:T(8,128)(2,1)S(1)}, bf16[2,256,128]{2,1,0:T(8,128)(2,1)S(1)}, u32[]{:S(2)}, u32[]{:S(2)}) collective-permute-start(bf16[2,256,128]{2,1,0:T(8,128)(2,1)S(1)} %get-tuple-element.232), channel_id=1, source_target_pairs={{0,1},{1,2},{2,3},{4,5},{5,6},{6,7},{8,9},{9,10},{10,11},{12,13},{... | collective-permute-start | bytes 393224 | tf_op jit(solution)/shard_map/while/body/eval_jaxpr/ppermute | solution.py:37
  334.1 1.9 collective-permute-done
  338.1 4.4 %collective-permute-start = (bf16[2,256,128]{2,1,0:T(8,128)(2,1)S(1)}, bf16[2,256,128]{2,1,0:T(8,128)(2,1)S(1)}, u32[]{:S(2)}, u32[]{:S(2)}) collective-permute-start(bf16[2,256,128]{2,1,0:T(8,128)(2,1)S(1)} %get-tuple-element.232), channel_id=1, source_target_pairs={{0,1},{1,2},{2,3},{4,5},{5,6},{6,7},{8,9},{9,10},{10,11},{12,13},{... | collective-permute-start | bytes 393224 | tf_op jit(solution)/shard_map/while/body/eval_jaxpr/ppermute | solution.py:37
  342.4 1.9 collective-permute-done
  345.3 1.0 convolution_add_fusion.4
  (76 shorter events, 15.7 us)
Async XLA Ops:
  6.5 1.5 copy-start
  6.5 73.6 %all-gather.3.cloned.1.call-start = ((), (), s32[]{:S(2)}) async-start(), calls=%async_computation | async-start | bytes 2359296 | tf_op jit(solution)/shard_map/all_gather | solution.py:100
  7.3 302.1 %all-gather.5.cloned.1.call-start = ((), (), s32[]{:S(2)}) async-start(), calls=%async_computation.1 | async-start | bytes 18874368 | tf_op jit(solution)/shard_map/all_gather | solution.py:99
  8.0 13.0 %collective-permute-start.1 = (bf16[1024,128]{1,0:T(8,128)(2,1)S(1)}, bf16[1024,128]{1,0:T(8,128)(2,1)S(1)}, u32[]{:S(2)}, u32[]{:S(2)}) collective-permute-start(bf16[1024,128]{1,0:T(8,128)(2,1)S(1)} %copy-done), channel_id=1, source_target_pairs={{0,4},{4,8},{8,12},{12,16},{16,20},{20,24},{24,28},{28,0},{1,5},{5... | collective-permute-start | bytes 786440 | tf_op jit(solution)/shard_map/ppermute | solution.py:25
  10.1 26.9 %collective-permute-start.5 = (bf16[1024,128]{1,0:T(8,128)(2,1)S(1)}, bf16[1024,128]{1,0:T(8,128)(2,1)S(1)}, u32[]{:S(2)}, u32[]{:S(2)}) collective-permute-start(bf16[1024,128]{1,0:T(8,128)(2,1)S(1)} %copy-done), channel_id=1, source_target_pairs={{4,0},{8,4},{12,8},{16,12},{20,16},{24,20},{28,24},{0,28},{5,1},{9... | collective-permute-start | bytes 786440 | tf_op jit(solution)/shard_map/ppermute | solution.py:27
  13.3 39.6 %copy-start.2 = (bf16[8192]{0:T(1024)(128)(2,1)S(1)}, bf16[8192]{0:T(1024)(128)(2,1)}, u32[]{:S(2)}) copy-start(bf16[8192]{0:T(1024)(128)(2,1)} %param.11) | copy-start | bytes 49156
  13.3 39.6 %copy-start.3 = (bf16[1024]{0:T(1024)(128)(2,1)S(1)}, bf16[1024]{0:T(1024)(128)(2,1)}, u32[]{:S(2)}) copy-start(bf16[1024]{0:T(1024)(128)(2,1)} %param.15) | copy-start | bytes 6148
  13.3 39.6 %copy-start.4 = (bf16[128]{0:T(256)(128)(2,1)S(1)}, bf16[128]{0:T(256)(128)(2,1)}, u32[]{:S(2)}) copy-start(bf16[128]{0:T(256)(128)(2,1)} %param.16) | copy-start | bytes 772
  13.3 39.6 %copy-start.5 = (bf16[128]{0:T(256)(128)(2,1)S(1)}, bf16[128]{0:T(256)(128)(2,1)}, u32[]{:S(2)}) copy-start(bf16[128]{0:T(256)(128)(2,1)} %param.17) | copy-start | bytes 772
  21.0 16.1 %collective-permute-start.2 = (bf16[1024,128]{1,0:T(8,128)(2,1)S(1)}, bf16[1024,128]{1,0:T(8,128)(2,1)S(1)}, u32[]{:S(2)}, u32[]{:S(2)}) collective-permute-start(bf16[1024,128]{1,0:T(8,128)(2,1)S(1)} %collective-permute-done.1), channel_id=1, source_target_pairs={{0,4},{4,8},{8,12},{12,16},{16,20},{20,24},{24,28},{28,0},{1,5},{5... | collective-permute-start | bytes 786440 | tf_op jit(solution)/shard_map/ppermute | solution.py:25
  37.1 13.0 %collective-permute-start.3 = (bf16[1024,128]{1,0:T(8,128)(2,1)S(1)}, bf16[1024,128]{1,0:T(8,128)(2,1)S(1)}, u32[]{:S(2)}, u32[]{:S(2)}) collective-permute-start(bf16[1024,128]{1,0:T(8,128)(2,1)S(1)} %collective-permute-done.2), channel_id=1, source_target_pairs={{0,4},{4,8},{8,12},{12,16},{16,20},{20,24},{24,28},{28,0},{1,5},{5... | collective-permute-start | bytes 786440 | tf_op jit(solution)/shard_map/ppermute | solution.py:25
  37.1 16.5 %collective-permute-start.6 = (bf16[1024,128]{1,0:T(8,128)(2,1)S(1)}, bf16[1024,128]{1,0:T(8,128)(2,1)}, u32[]{:S(2)}, u32[]{:S(2)}) collective-permute-start(bf16[1024,128]{1,0:T(8,128)(2,1)S(1)} %collective-permute-done.5), channel_id=1, source_target_pairs={{4,0},{8,4},{12,8},{16,12},{20,16},{24,20},{28,24},{0,28},{5,1},{9... | collective-permute-start | bytes 786440 | tf_op jit(solution)/shard_map/ppermute | solution.py:27
  50.0 12.8 %copy-start.1 = (bf16[1024,128]{1,0:T(8,128)(2,1)}, bf16[1024,128]{1,0:T(8,128)(2,1)S(1)}, u32[]{:S(2)}) copy-start(bf16[1024,128]{1,0:T(8,128)(2,1)S(1)} %collective-permute-done.3) | copy-start | bytes 786436
  50.0 19.5 %collective-permute-start.4 = (bf16[1024,128]{1,0:T(8,128)(2,1)S(1)}, bf16[1024,128]{1,0:T(8,128)(2,1)}, u32[]{:S(2)}, u32[]{:S(2)}) collective-permute-start(bf16[1024,128]{1,0:T(8,128)(2,1)S(1)} %collective-permute-done.3), channel_id=1, source_target_pairs={{0,4},{4,8},{8,12},{12,16},{16,20},{20,24},{24,28},{28,0},{1,5},{5... | collective-permute-start | bytes 786440 | tf_op jit(solution)/shard_map/ppermute | solution.py:25
  53.6 19.5 %collective-permute-start.7 = (bf16[1024,128]{1,0:T(8,128)(2,1)}, bf16[1024,128]{1,0:T(8,128)(2,1)S(1)}, u32[]{:S(2)}, u32[]{:S(2)}) collective-permute-start(bf16[1024,128]{1,0:T(8,128)(2,1)} %collective-permute-done.6), channel_id=1, source_target_pairs={{4,0},{8,4},{12,8},{16,12},{20,16},{24,20},{28,24},{0,28},{5,1},{9... | collective-permute-start | bytes 786440 | tf_op jit(solution)/shard_map/ppermute | solution.py:27
  321.8 6.0 %collective-permute-start = (bf16[2,256,128]{2,1,0:T(8,128)(2,1)S(1)}, bf16[2,256,128]{2,1,0:T(8,128)(2,1)S(1)}, u32[]{:S(2)}, u32[]{:S(2)}) collective-permute-start(bf16[2,256,128]{2,1,0:T(8,128)(2,1)S(1)} %get-tuple-element.232), channel_id=1, source_target_pairs={{0,1},{1,2},{2,3},{4,5},{5,6},{6,7},{8,9},{9,10},{10,11},{12,13},{... | collective-permute-start | bytes 393224 | tf_op jit(solution)/shard_map/while/body/eval_jaxpr/ppermute | solution.py:37
  329.8 6.3 %collective-permute-start = (bf16[2,256,128]{2,1,0:T(8,128)(2,1)S(1)}, bf16[2,256,128]{2,1,0:T(8,128)(2,1)S(1)}, u32[]{:S(2)}, u32[]{:S(2)}) collective-permute-start(bf16[2,256,128]{2,1,0:T(8,128)(2,1)S(1)} %get-tuple-element.232), channel_id=1, source_target_pairs={{0,1},{1,2},{2,3},{4,5},{5,6},{6,7},{8,9},{9,10},{10,11},{12,13},{... | collective-permute-start | bytes 393224 | tf_op jit(solution)/shard_map/while/body/eval_jaxpr/ppermute | solution.py:37
  338.1 6.3 %collective-permute-start = (bf16[2,256,128]{2,1,0:T(8,128)(2,1)S(1)}, bf16[2,256,128]{2,1,0:T(8,128)(2,1)S(1)}, u32[]{:S(2)}, u32[]{:S(2)}) collective-permute-start(bf16[2,256,128]{2,1,0:T(8,128)(2,1)S(1)} %get-tuple-element.232), channel_id=1, source_target_pairs={{0,1},{1,2},{2,3},{4,5},{5,6},{6,7},{8,9},{9,10},{10,11},{12,13},{... | collective-permute-start | bytes 393224 | tf_op jit(solution)/shard_map/while/body/eval_jaxpr/ppermute | solution.py:37
Sparse Core Ops, SparseCore 0:
  9.5 70.6 all-gather.2
  82.3 226.9 all-gather.4
